TPU v7x, 32 devices: a whole 2x2x4 slice. The times are simulated.
32 devices in a mesh: ri: 16 (over z, y, core), rj: 2 (over x).
Axes of the slice: x: 2, y: 2, z: 4, core: 2. Of those that a mesh axis runs over, the one named last changes fastest.
Arguments:
- pair: bfloat16 [64, 512, 512], P(None, 'ri', 'rj'), may hold values from -6 to 6
- conv1_weight: bfloat16 [3, 3, 64, 64], replicated, may hold values from -0.25 to 0.25
- conv1_bias: float32 [64], replicated, may hold values from -3 to 3
- conv2_weight: bfloat16 [3, 3, 64, 64], replicated, may hold values from -0.25 to 0.25
- conv2_bias: float32 [64], replicated, may hold values from -3 to 3
- head_weight: bfloat16 [64, 37], replicated, may hold values from -60 to 60, as said below
- head_bias: float32 [37], replicated, may hold values from -4 to 4
- bins: int32 [512, 512], P('ri', 'rj'), may hold values from 0 to 36
- mask: int32 [512], replicated, may hold values from 0 to 1, as said below
Outputs:
- grad_pair: bfloat16 [64, 512, 512], P(None, 'ri', 'rj')
- grad_conv1_weight: float32 [3, 3, 64, 64], replicated
- grad_conv1_bias: float32 [64], replicated
- grad_conv2_weight: float32 [3, 3, 64, 64], replicated
- grad_conv2_bias: float32 [64], replicated
- grad_head_weight: float32 [64, 37], replicated
- grad_head_bias: float32 [37], replicated
Inputs may be any that keep to these rules, and one draw needn't show every extreme that they name: `mask`: residue 0 is always valid; all valid residues lie before some position that is at least 256. `head_weight`: some bins' weights may reach tens in magnitude, so that logits may reach hundreds.
All inputs are finite; a program needn't handle non-finite values.
Results may differ from a plain program's by a relative error of at most 0.012.
The roundings to bfloat16 on the way count: a program that leaves them out, or rounds other values in their place, can miss the bound.
Values may be sent and summed in bfloat16 or wider, within the bound.
A program may use at most 128 MiB of HBM per device.

v0:
```python
import jax
import jax.numpy as jnp
from jax import lax
from jax.sharding import PartitionSpec as P

KERNEL_TAPS = 3
DILATION_RATE = 8


def with_halo(cells, sides, width):
    for axis, dim in sides:
        count = lax.axis_size(axis)
        ends = count - 1
        head = lax.slice_in_dim(cells, 0, width, axis=dim)
        tail = lax.slice_in_dim(cells, cells.shape[dim] - width, cells.shape[dim], axis=dim)
        cells = jnp.concatenate(
            [
                lax.ppermute(tail, axis, [(i, (i + 1) % count) for i in range(ends)]),
                cells,
                lax.ppermute(head, axis, [((i + 1) % count, i) for i in range(ends)]),
            ],
            axis=dim,
        )
    return cells


def activate(value):
    return jnp.where(value > 0, value, jnp.expm1(jnp.minimum(value, 0.0)))


def activate_slope(value):
    return jnp.where(value > 0, 1.0, jnp.exp(jnp.minimum(value, 0.0)))


def with_rims(residual_block):
    return with_halo(residual_block, (("ri", 1), ("rj", 2)), DILATION_RATE * (KERNEL_TAPS // 2))


def dilated(padded_field, weight):
    return lax.conv_general_dilated(
        padded_field[None],
        weight,
        (1, 1),
        [(0, 0), (0, 0)],
        rhs_dilation=(DILATION_RATE, DILATION_RATE),
        dimension_numbers=("NCHW", "HWIO", "NCHW"),
        preferred_element_type=jnp.float32,
    )[0]


def flipped(weight):
    return jnp.transpose(weight[::-1, ::-1], (0, 1, 3, 2))


def tap_sums(padded_field, grad):
    row_extent = grad.shape[1]
    column_extent = grad.shape[2]
    tap_rows = []
    for row_stride in range(KERNEL_TAPS):
        across = []
        for column_stride in range(KERNEL_TAPS):
            sliding_window = padded_field[
                :,
                DILATION_RATE * row_stride : DILATION_RATE * row_stride + row_extent,
                DILATION_RATE * column_stride : DILATION_RATE * column_stride + column_extent,
            ]
            across.append(
                jnp.einsum("cij,dij->cd", sliding_window, grad, preferred_element_type=jnp.float32)
            )
        tap_rows.append(jnp.stack(across))
    return jnp.stack(tap_rows)


def mirror(residual_block, first_move, second_move):
    chan_count, row_count, col_count = residual_block.shape
    col_groups = lax.axis_size("rj")
    row_groups = lax.axis_size("ri") // col_groups
    depth_rows = row_count // col_groups
    sectioned = first_move(residual_block.reshape(chan_count, col_groups, depth_rows, col_count))
    sectioned = sectioned.reshape(chan_count, depth_rows, col_groups * col_count)
    arrived = second_move(sectioned)
    arrived = arrived.reshape(chan_count, row_groups, depth_rows, col_groups, row_count)
    return jnp.transpose(arrived, (0, 4, 1, 3, 2)).reshape(chan_count, row_count, col_count)


def feature_first(sectioned):
    return lax.all_to_all(sectioned, "rj", split_axis=1, concat_axis=3, tiled=True)


def feature_second(sectioned):
    return lax.all_to_all(
        lax.all_to_all(sectioned, "ri", split_axis=2, concat_axis=1, tiled=True),
        "rj",
        split_axis=1,
        concat_axis=2,
        tiled=True,
    )


def slope_first(sectioned):
    return lax.all_to_all(sectioned, "rj", split_axis=1, concat_axis=3, tiled=True)


def slope_second(sectioned):
    return lax.all_to_all(
        lax.all_to_all(sectioned, "ri", split_axis=2, concat_axis=1, tiled=True),
        "rj",
        split_axis=1,
        concat_axis=2,
        tiled=True,
    )


def on_device(
    pair, conv1_weight, conv1_bias, conv2_weight, conv2_bias, head_weight, head_bias, bins, mask
):
    row_count = pair.shape[1]
    col_count = pair.shape[2]
    row_valid = lax.dynamic_slice_in_dim(mask, lax.axis_index("ri") * row_count, row_count).astype(
        jnp.float32
    )
    col_valid = lax.dynamic_slice_in_dim(mask, lax.axis_index("rj") * col_count, col_count).astype(
        jnp.float32
    )
    pair_mask = row_valid[:, None] * col_valid[None, :]
    n_valid = jnp.sum(mask.astype(jnp.float32))
    pair_pad = with_rims(pair)
    inner = dilated(pair_pad, conv1_weight) + conv1_bias[:, None, None]
    inner_act = activate(inner).astype(jnp.bfloat16)
    act_pad = with_rims(inner_act)
    outer = dilated(act_pad, conv2_weight) + conv2_bias[:, None, None]
    summed = pair.astype(jnp.float32) + outer
    hidden = (pair_mask[None] * activate(summed)).astype(jnp.bfloat16)
    mirrored = mirror(hidden, feature_first, feature_second)
    logits = 0.5 * (
        jnp.einsum("ck,cij->kij", head_weight, hidden, preferred_element_type=jnp.float32)
        + jnp.einsum("ck,cij->kij", head_weight, mirrored, preferred_element_type=jnp.float32)
    )
    logits = logits + head_bias[:, None, None]
    peak_logit = jnp.max(logits, axis=0, keepdims=True)
    powered = jnp.exp(logits - peak_logit)
    chance = powered / jnp.sum(powered, axis=0, keepdims=True)
    bin_ids = jnp.arange(head_weight.shape[1], dtype=jnp.int32)[:, None, None]
    onehot = (bins[None, :, :] == bin_ids).astype(jnp.float32)
    error = pair_mask[None] * (chance - onehot)
    symmetric = 0.5 * (hidden.astype(jnp.float32) + mirrored.astype(jnp.float32))
    head_term = jnp.einsum(
        "cij,kij->ck",
        symmetric,
        error,
        precision=lax.Precision.HIGHEST,
        preferred_element_type=jnp.float32,
    )
    head_bias_term = jnp.sum(error, axis=(1, 2))
    weight_wide = head_weight.astype(jnp.float32)
    slope = jnp.einsum(
        "ck,kij->cij",
        weight_wide,
        error,
        precision=lax.Precision.HIGHEST,
        preferred_element_type=jnp.float32,
    )
    slope_mirrored = mirror(slope, slope_first, slope_second)
    half_slope = 0.5 * (slope + slope_mirrored)
    outer_grad = half_slope * pair_mask[None] * activate_slope(summed)
    outer_half = outer_grad.astype(jnp.bfloat16)
    conv2_term = tap_sums(act_pad, outer_half)
    conv2_bias_term = jnp.sum(outer_grad, axis=(1, 2))
    inner_grad = dilated(with_rims(outer_half), flipped(conv2_weight)) * activate_slope(inner)
    inner_half = inner_grad.astype(jnp.bfloat16)
    conv1_term = tap_sums(pair_pad, inner_half)
    conv1_bias_term = jnp.sum(inner_grad, axis=(1, 2))
    grad_pair = (outer_grad + dilated(with_rims(inner_half), flipped(conv1_weight))).astype(
        jnp.bfloat16
    )
    totals = lax.psum(
        (conv1_term, conv1_bias_term, conv2_term, conv2_bias_term, head_term, head_bias_term),
        ("ri", "rj"),
    )
    return (
        grad_pair,
        totals[0] / n_valid,
        totals[1] / n_valid,
        totals[2] / n_valid,
        totals[3] / n_valid,
        totals[4] / n_valid,
        totals[5] / n_valid,
    )


def solution(mesh):
    return jax.shard_map(
        on_device,
        mesh=mesh,
        in_specs=(P(None, "ri", "rj"), P(), P(), P(), P(), P(), P(), P("ri", "rj"), P()),
        out_specs=(P(None, "ri", "rj"), P(), P(), P(), P(), P(), P()),
        check_vma=False,
    )
```

profile of v0, /device:TPU:0, one launch (start us, length us, event | category | flops | bytes accessed | tf_op | source)
XLA Modules:
  0.0 720.4 jit_solution(4406372204763931923)
XLA Ops:
  33.1 6.0 copy.145
  58.7 5.9 collective-permute-start.4
  91.3 6.0 copy.154
  117.2 16.0 %all_to_all.96 = bf16[64,2,16,256]{3,2,0,1:T(8,128)(2,1)} all-to-all(bf16[64,2,16,256]{3,2,0,1:T(8,128)(2,1)S(1)} %copy.159), channel_id=1, replica_groups=mesh['ri'=16,'rj'=2] {'rj'}, dimensions={1} | all-to-all | bytes 2097152 | tf_op jit(solution)/shard_map/all_to_all | solution.py:87
  143.0 37.1 %all_to_all.97 = bf16[16,2,16384]{2,1,0:T(2,128)(2,1)} all-to-all(bf16[16,2,16384]{2,1,0:T(2,128)(2,1)} %reshape.155), channel_id=1, replica_groups=mesh['ri'=16,'rj'=2] {'ri'}, dimensions={0} | all-to-all | bytes 2097152 | tf_op jit(solution)/shard_map/all_to_all | solution.py:92
  199.0 12.2 %all-to-all-done.2 = bf16[2,2,131072]{2,1,0:T(2,128)(2,1)} async-done(((bf16[2,2,131072]{2,1,0:T(2,128)(2,1)}), bf16[2,2,131072]{2,1,0:T(2,128)(2,1)}, u32[]{:S(2)}, u32[]{:S(2)}) %all-to-all-start.2) | async-done | bytes 1048608 | tf_op jit(solution)/shard_map/all_to_all | solution.py:91
  227.6 29.0 %all_to_all.98 = f32[64,2,16,256]{3,2,0,1:T(8,128)} all-to-all(f32[64,2,16,256]{3,2,0,1:T(8,128)S(1)} %copy.167), channel_id=1, replica_groups=mesh['ri'=16,'rj'=2] {'rj'}, dimensions={1} | all-to-all | bytes 4194304 | tf_op jit(solution)/shard_map/all_to_all | solution.py:101
  256.6 5.3 copy.208
  261.9 5.5 reshape.159
  273.1 39.8 %all-to-all-done.4 = f32[16,1,32768]{2,1,0:T(1,128)} async-done(((f32[16,1,32768]{2,1,0:T(1,128)}), f32[16,1,32768]{2,1,0:T(1,128)}, u32[]{:S(2)}, u32[]{:S(2)}) %all-to-all-start.4) | async-done | bytes 2097184 | tf_op jit(solution)/shard_map/all_to_all | solution.py:106
  313.4 8.7 %reduce = f32[16,32768]{1,0:T(8,128)} reduce(f32[16,1,32768]{2,1,0:T(1,128)} %all-to-all-done.4, f32[]{:T(128)} %broadcast.123), dimensions={1}, to_apply=%all_to_all.83.reduce_sub_computation | reduce | bytes 4194308 | tf_op jit(solution)/shard_map/all_to_all | solution.py:106
  326.4 5.5 copy.171
  331.9 5.2 reshape.161
  356.8 11.2 %all-to-all-done.5 = f32[2,1,262144]{2,1,0:T(1,128)} async-done(((f32[2,1,262144]{2,1,0:T(1,128)}), f32[2,1,262144]{2,1,0:T(1,128)}, u32[]{:S(2)}, u32[]{:S(2)}) %all-to-all-start.5) | async-done | bytes 2097184 | tf_op jit(solution)/shard_map/all_to_all | solution.py:105
  368.0 9.5 %reduce.1 = f32[2,262144]{1,0:T(2,128)} reduce(f32[2,1,262144]{2,1,0:T(1,128)} %all-to-all-done.5, f32[]{:T(128)} %broadcast.123), dimensions={1}, to_apply=%all_to_all.87.reduce_sub_computation | reduce | bytes 4194308 | tf_op jit(solution)/shard_map/all_to_all | solution.py:105
  377.5 5.9 reshape.162
  383.4 6.6 copy.173
  436.5 6.0 copy.179
  446.4 5.5 broadcast_select_fusion.1
  474.1 5.2 collective-permute-start.12
  480.6 48.6 %all-reduce = (f32[64]{0:T(128)S(1)}, f32[64]{0:T(128)S(1)}, f32[64,37]{0,1:T(8,128)S(1)}, f32[37]{0:T(128)}) all-reduce(f32[64]{0:T(128)} %get-tuple-element.43, f32[64]{0:T(128)} %get-tuple-element.41, f32[64,37]{0,1:T(8,128)} %fusion.91, f32[37]{0:T(128)} %fusion.142), channel_id=1, replica_groups=mesh['ri'=16,'rj'=2] {'ri','rj'}, use_global_device_ids=true, to_apply=%region_5.6 | all-reduce | flops 2533 | bytes 20264 | tf_op jit(solution)/shard_map/psum | solution.py:176
  536.9 126.6 %all-reduce.4.cloned.1.call-done = (f32[3,3,64,64]{3,2,1,0:T(8,128)}, f32[3,3,64,64]{3,2,1,0:T(8,128)}) async-done(((f32[3,3,64,64]{3,2,1,0:T(8,128)}, f32[3,3,64,64]{3,2,1,0:T(8,128)}), (f32[3,3,64,64]{3,2,1,0:T(8,128)}, f32[3,3,64,64]{3,2,1,0:T(8,128)})) %all-reduce.4.cloned.1.call-update) | async-done | bytes 294928 | tf_op jit(solution)/shard_map/psum | solution.py:176
  685.2 6.0 copy.188
  695.3 5.5 broadcast_select_fusion
  (213 shorter events, 286.6 us)
Async XLA Ops:
  7.2 93.9 %copy-start = (bf16[3,3,64,64]{3,2,1,0:T(8,128)(2,1)S(1)}, bf16[3,3,64,64]{3,2,1,0:T(8,128)(2,1)}, u32[]{:S(2)}) copy-start(bf16[3,3,64,64]{3,2,1,0:T(8,128)(2,1)} %param.12) | copy-start | bytes 221188
  9.2 3.7 collective-permute-start
  11.5 5.5 collective-permute-start.1
  18.5 5.6 collective-permute-start.2
  22.2 6.6 collective-permute-start.3
  58.7 10.0 %collective-permute-start.4 = (bf16[64,8,256]{2,0,1:T(8,128)(2,1)}, bf16[64,8,256]{2,0,1:T(8,128)(2,1)}, u32[]{:S(2)}, u32[]{:S(2)}) collective-permute-start(bf16[64,8,256]{2,0,1:T(8,128)(2,1)} %get-tuple-element.59), channel_id=1, source_target_pairs={{0,2},{2,4},{4,6},{6,8},{8,10},{10,12},{12,14},{14,16},{16,18},{18... | collective-permute-start | bytes 786440 | tf_op jit(solution)/shard_map/ppermute | solution.py:18
  64.7 4.1 collective-permute-start.5
  73.6 7.0 collective-permute-start.6
  78.0 6.8 collective-permute-start.7
  116.6 16.6 %copy-start.6 = (bf16[64,32,256]{2,0,1:T(8,128)(2,1)}, bf16[64,32,256]{2,0,1:T(8,128)(2,1)S(1)}, u32[]{:S(2)}) copy-start(bf16[64,32,256]{2,0,1:T(8,128)(2,1)S(1)} %fusion.40) | copy-start | bytes 3145732
  191.9 19.3 %all-to-all-start.2 = ((bf16[2,2,131072]{2,1,0:T(2,128)(2,1)}), bf16[2,2,131072]{2,1,0:T(2,128)(2,1)}, u32[]{:S(2)}, u32[]{:S(2)}) async-start(bf16[2,2,131072]{2,1,0:T(2,128)(2,1)} %reshape.157), calls=%async_computation.2 | async-start | bytes 2097152 | tf_op jit(solution)/shard_map/all_to_all | solution.py:91
  267.4 45.5 %all-to-all-start.4 = ((f32[16,1,32768]{2,1,0:T(1,128)}), f32[16,1,32768]{2,1,0:T(1,128)}, u32[]{:S(2)}, u32[]{:S(2)}) async-start(f32[16,1,32768]{2,1,0:T(1,128)} %reshape.159), calls=%async_computation.4 | async-start | bytes 4194304 | tf_op jit(solution)/shard_map/all_to_all | solution.py:106
  337.1 31.0 %all-to-all-start.5 = ((f32[2,1,262144]{2,1,0:T(1,128)}), f32[2,1,262144]{2,1,0:T(1,128)}, u32[]{:S(2)}, u32[]{:S(2)}) async-start(f32[2,1,262144]{2,1,0:T(1,128)} %reshape.161), calls=%async_computation.5 | async-start | bytes 4194304 | tf_op jit(solution)/shard_map/all_to_all | solution.py:105
  341.9 321.6 %all-reduce.4.cloned.1.call-start = ((), (), s32[]{:S(2)}) async-start(), calls=%async_computation.6 | async-start | bytes 1179648 | tf_op jit(solution)/shard_map/psum | solution.py:176
  406.2 7.3 %collective-permute-start.8 = (bf16[64,8,256]{2,0,1:T(8,128)(2,1)S(1)}, bf16[64,8,256]{2,0,1:T(8,128)(2,1)S(1)}, u32[]{:S(2)}, u32[]{:S(2)}) collective-permute-start(bf16[64,8,256]{2,0,1:T(8,128)(2,1)S(1)} %get-tuple-element.57), channel_id=1, source_target_pairs={{0,2},{2,4},{4,6},{6,8},{8,10},{10,12},{12,14},{14,16},{16,18},{18... | collective-permute-start | bytes 786440 | tf_op jit(solution)/shard_map/ppermute | solution.py:18
  408.0 6.5 collective-permute-start.9
  418.4 7.7 %collective-permute-start.10 = (bf16[64,48,8]{0,2,1:T(8,128)(2,1)}, bf16[64,48,8]{0,2,1:T(8,128)(2,1)}, u32[]{:S(2)}, u32[]{:S(2)}) collective-permute-start(bf16[64,48,8]{0,2,1:T(8,128)(2,1)} %copy.175), channel_id=1, source_target_pairs={{0,1},{2,3},{4,5},{6,7},{8,9},{10,11},{12,13},{14,15},{16,17},{18,... | collective-permute-start | bytes 147464 | tf_op jit(solution)/shard_map/ppermute | solution.py:18
  423.1 6.8 collective-permute-start.11
  473.3 60.7 %copy-start.11 = (bf16[64,32,256]{2,0,1:T(8,128)(2,1)S(1)}, bf16[64,32,256]{2,0,1:T(8,128)(2,1)}, u32[]{:S(2)}) copy-start(bf16[64,32,256]{2,0,1:T(8,128)(2,1)} %copy-done.10) | copy-start | bytes 3145732
  473.3 60.7 %copy-start.19 = (bf16[64,8,256]{2,0,1:T(8,128)(2,1)S(1)}, bf16[64,8,256]{2,0,1:T(8,128)(2,1)}, u32[]{:S(2)}) copy-start(bf16[64,8,256]{2,0,1:T(8,128)(2,1)} %copy-done.18) | copy-start | bytes 786436
  474.1 191.7 %collective-permute-start.12 = (bf16[64,8,256]{2,0,1:T(8,128)(2,1)}, bf16[64,8,256]{2,0,1:T(8,128)(2,1)S(1)}, u32[]{:S(2)}, u32[]{:S(2)}) collective-permute-start(bf16[64,8,256]{2,0,1:T(8,128)(2,1)} %get-tuple-element.55), channel_id=1, source_target_pairs={{0,2},{2,4},{4,6},{6,8},{8,10},{10,12},{12,14},{14,16},{16,18},{18... | collective-permute-start | bytes 786440 | tf_op jit(solution)/shard_map/ppermute | solution.py:18
  479.3 186.5 %collective-permute-start.13 = (bf16[64,8,256]{2,0,1:T(8,128)(2,1)S(1)}, bf16[64,8,256]{2,0,1:T(8,128)(2,1)S(1)}, u32[]{:S(2)}, u32[]{:S(2)}) collective-permute-start(bf16[64,8,256]{2,0,1:T(8,128)(2,1)S(1)} %get-tuple-element.56), channel_id=1, source_target_pairs={{2,0},{4,2},{6,4},{8,6},{10,8},{12,10},{14,12},{16,14},{18,16},{20... | collective-permute-start | bytes 786440 | tf_op jit(solution)/shard_map/ppermute | solution.py:20
  670.1 7.2 %collective-permute-start.14 = (bf16[64,48,8]{0,2,1:T(8,128)(2,1)S(1)}, bf16[64,48,8]{0,2,1:T(8,128)(2,1)S(1)}, u32[]{:S(2)}, u32[]{:S(2)}) collective-permute-start(bf16[64,48,8]{0,2,1:T(8,128)(2,1)S(1)} %copy.184), channel_id=1, source_target_pairs={{0,1},{2,3},{4,5},{6,7},{8,9},{10,11},{12,13},{14,15},{16,17},{18,... | collective-permute-start | bytes 147464 | tf_op jit(solution)/shard_map/ppermute | solution.py:18
  673.7 6.6 collective-permute-start.15
  (27 other events, 74.8 us)
Sparse Core Ops, SparseCore 0:
  535.4 128.0 all-reduce.3
where the time goes:
time: 726 us; the launch traced here: 720 us
  waiting for transfers between devices  205 us (28%)
  local copies, waits for them, and re-layouts  188 us (26%)
  blocking collectives  131 us (18%)
  other arithmetic  78.8 us (11%)
  starting transfers between devices  51.8 us (7%)
  matrix products  51.3 us (7%)
  between operations  15 us (2%)
    psum x1, waiting for transfers between devices, on_device(): lax.psum((conv1_term, conv1_bias_term, conv2_term, conv2_bias_term, head_...  127 us
    unnamed x78, local copies, waits for them, and re-layouts  67.4 us
    psum x1, blocking collectives, on_device(): lax.psum((conv1_term, conv1_bias_term, conv2_term, conv2_bias_term, head_...  48.6 us
    all_to_all x1, waiting for transfers between devices, slope_second(): lax.all_to_all(sectioned, 'ri', split_axis=2, concat_axis=1, tiled=True)  39.8 us
    all_to_all x1, blocking collectives, feature_second(): lax.all_to_all(sectioned, 'ri', split_axis=2, concat_axis=1, tiled=True)  37.1 us
    conv_general_dilated x16, local copies, waits for them, and re-layouts, dilated(): lax.conv_general_dilated(padded_field[None], weight, (1, 1), [(0, 0), (0,...  30.2 us
    all_to_all x1, blocking collectives, slope_first(): lax.all_to_all(sectioned, 'rj', split_axis=1, concat_axis=3, tiled=True)  29 us
    ppermute x8, starting transfers between devices, with_halo(): lax.ppermute(tail, axis, [(i, (i + 1) % count) for i in range(ends)])  27.1 us
  transfers between devices with their start and end apart: 20, of which 11 were waited for; matrix products, arithmetic and copies ran while one was open for 7% of the time, Pallas kernels for 0%

commit v1 on v0

--- a/solution.py
+++ b/solution.py
@@ -174,8 +174,11 @@
         jnp.bfloat16
     )
     totals = lax.psum(
-        (conv1_term, conv1_bias_term, conv2_term, conv2_bias_term, head_term, head_bias_term),
-        ("ri", "rj"),
+        lax.psum(
+            (conv1_term, conv1_bias_term, conv2_term, conv2_bias_term, head_term, head_bias_term),
+            "rj",
+        ),
+        "ri",
     )
     return (
         grad_pair,

time: 726 us -> 671 us (0.924)
  waiting for transfers between devices: 205 us -> 132 us
  blocking collectives: 131 us -> 154 us
    psum x1, waiting for transfers between devices: 127 us -> 0.01 us  [on_device(): lax.psum((conv1_term, conv1_bias_term, conv2_term, conv2_bias_term, head_...]
    psum x0 -> x1, blocking collectives: none -> 63 us  [on_device(): lax.psum(lax.psum((conv1_term, conv1_bias_term, conv2_term, conv2_bias_te...]
    psum x0 -> x1, waiting for transfers between devices: none -> 54 us  [on_device(): lax.psum(lax.psum((conv1_term, conv1_bias_term, conv2_term, conv2_bias_te...]
    psum x1, blocking collectives: 48.6 us -> 9.22 us  [on_device(): lax.psum((conv1_term, conv1_bias_term, conv2_term, conv2_bias_term, head_...]
    unnamed x78 -> x80, local copies, waits for them, and re-layouts: 67.4 us -> 68.6 us
  transfers between devices with their start and end apart: 20 -> 21, of which waited for: 11 -> 11; matrix products, arithmetic and copies ran while one was open for 7% -> 12% of each run, Pallas kernels for 0% -> 0%
where the time goes in v1:
time: 671 us; the launch traced here: 665 us
  local copies, waits for them, and re-layouts  189 us (28%)
  blocking collectives  154 us (23%)
  waiting for transfers between devices  132 us (20%)
  other arithmetic  78.1 us (12%)
  starting transfers between devices  50.9 us (8%)
  matrix products  45.7 us (7%)
  between operations  15.1 us (2%)
    unnamed x80, local copies, waits for them, and re-layouts  68.6 us
    psum x1, blocking collectives, on_device(): lax.psum(lax.psum((conv1_term, conv1_bias_term, conv2_term, conv2_bias_te...  63 us
    psum x1, waiting for transfers between devices, on_device(): lax.psum(lax.psum((conv1_term, conv1_bias_term, conv2_term, conv2_bias_te...  54 us
    all_to_all x1, waiting for transfers between devices, slope_second(): lax.all_to_all(sectioned, 'ri', split_axis=2, concat_axis=1, tiled=True)  39.8 us
    all_to_all x1, blocking collectives, feature_second(): lax.all_to_all(sectioned, 'ri', split_axis=2, concat_axis=1, tiled=True)  37.1 us
    conv_general_dilated x16, local copies, waits for them, and re-layouts, dilated(): lax.conv_general_dilated(padded_field[None], weight, (1, 1), [(0, 0), (0,...  30.2 us
    all_to_all x1, blocking collectives, slope_first(): lax.all_to_all(sectioned, 'rj', split_axis=1, concat_axis=3, tiled=True)  29 us
    ppermute x8, starting transfers between devices, with_halo(): lax.ppermute(tail, axis, [(i, (i + 1) % count) for i in range(ends)])  26.2 us
  transfers between devices with their start and end apart: 21, of which 11 were waited for; matrix products, arithmetic and copies ran while one was open for 12% of the time, Pallas kernels for 0%

profile of v1, /device:TPU:0, one launch (start us, length us, event | category | flops | bytes accessed | tf_op | source)
XLA Modules:
  0.0 665.1 jit_solution(9913654682579900262)
XLA Ops:
  33.1 6.0 copy.145
  58.7 6.0 collective-permute-start.4
  91.3 6.0 copy.154
  117.1 16.1 %all_to_all.96 = bf16[64,2,16,256]{3,2,0,1:T(8,128)(2,1)} all-to-all(bf16[64,2,16,256]{3,2,0,1:T(8,128)(2,1)S(1)} %copy.159), channel_id=1, replica_groups=mesh['ri'=16,'rj'=2] {'rj'}, dimensions={1} | all-to-all | bytes 2097152 | tf_op jit(solution)/shard_map/all_to_all | solution.py:87
  142.9 37.1 %all_to_all.97 = bf16[16,2,16384]{2,1,0:T(2,128)(2,1)} all-to-all(bf16[16,2,16384]{2,1,0:T(2,128)(2,1)} %reshape.155), channel_id=1, replica_groups=mesh['ri'=16,'rj'=2] {'ri'}, dimensions={0} | all-to-all | bytes 2097152 | tf_op jit(solution)/shard_map/all_to_all | solution.py:92
  198.9 12.2 %all-to-all-done.2 = bf16[2,2,131072]{2,1,0:T(2,128)(2,1)} async-done(((bf16[2,2,131072]{2,1,0:T(2,128)(2,1)}), bf16[2,2,131072]{2,1,0:T(2,128)(2,1)}, u32[]{:S(2)}, u32[]{:S(2)}) %all-to-all-start.2) | async-done | bytes 1048608 | tf_op jit(solution)/shard_map/all_to_all | solution.py:91
  227.6 29.0 %all_to_all.98 = f32[64,2,16,256]{3,2,0,1:T(8,128)} all-to-all(f32[64,2,16,256]{3,2,0,1:T(8,128)S(1)} %copy.167), channel_id=1, replica_groups=mesh['ri'=16,'rj'=2] {'rj'}, dimensions={1} | all-to-all | bytes 4194304 | tf_op jit(solution)/shard_map/all_to_all | solution.py:101
  256.6 5.3 copy.208
  261.8 5.5 reshape.159
  273.1 39.8 %all-to-all-done.4 = f32[16,1,32768]{2,1,0:T(1,128)} async-done(((f32[16,1,32768]{2,1,0:T(1,128)}), f32[16,1,32768]{2,1,0:T(1,128)}, u32[]{:S(2)}, u32[]{:S(2)}) %all-to-all-start.4) | async-done | bytes 2097184 | tf_op jit(solution)/shard_map/all_to_all | solution.py:106
  313.4 8.7 %reduce = f32[16,32768]{1,0:T(8,128)} reduce(f32[16,1,32768]{2,1,0:T(1,128)} %all-to-all-done.4, f32[]{:T(128)} %broadcast.123), dimensions={1}, to_apply=%all_to_all.83.reduce_sub_computation | reduce | bytes 4194308 | tf_op jit(solution)/shard_map/all_to_all | solution.py:106
  326.3 5.5 copy.171
  356.8 11.2 %all-to-all-done.5 = f32[2,1,262144]{2,1,0:T(1,128)} async-done(((f32[2,1,262144]{2,1,0:T(1,128)}), f32[2,1,262144]{2,1,0:T(1,128)}, u32[]{:S(2)}, u32[]{:S(2)}) %all-to-all-start.5) | async-done | bytes 2097184 | tf_op jit(solution)/shard_map/all_to_all | solution.py:105
  368.0 9.5 %reduce.1 = f32[2,262144]{1,0:T(2,128)} reduce(f32[2,1,262144]{2,1,0:T(1,128)} %all-to-all-done.5, f32[]{:T(128)} %broadcast.123), dimensions={1}, to_apply=%all_to_all.87.reduce_sub_computation | reduce | bytes 4194308 | tf_op jit(solution)/shard_map/all_to_all | solution.py:105
  377.4 5.8 reshape.162
  383.3 6.6 copy.173
  436.3 6.0 copy.179
  446.2 5.5 broadcast_select_fusion.1
  470.0 5.4 collective-permute-start.12
  478.5 9.2 %all-reduce.2 = (f32[64]{0:T(128)S(1)}, f32[64]{0:T(128)S(1)}, f32[64,37]{0,1:T(8,128)S(1)}, f32[37]{0:T(128)S(1)}) all-reduce(f32[64]{0:T(128)S(1)} %copy-done.25, f32[64]{0:T(128)S(1)} %copy-done.24, f32[64,37]{0,1:T(8,128)S(1)} %copy-done.22, f32[37]{0:T(128)S(1)} %copy-done.23), channel_id=1, replica_groups=mesh['ri'=16,'rj'=2] {'rj'}, use_global_device_ids=true, to_apply=%region_6.7 | all-reduce | flops 2533 | bytes 20264 | tf_op jit(solution)/shard_map/psum | solution.py:177
  487.8 63.0 %all-reduce = (f32[64]{0:T(128)S(1)}, f32[64]{0:T(128)S(1)}, f32[64,37]{0,1:T(8,128)S(1)}, f32[37]{0:T(128)}) all-reduce(f32[64]{0:T(128)S(1)} %get-tuple-element.41, f32[64]{0:T(128)S(1)} %get-tuple-element.42, f32[64,37]{0,1:T(8,128)S(1)} %get-tuple-element.43, f32[37]{0:T(128)S(1)} %get-tuple-element.44), channel_id=1, replica_groups=mesh['ri'=16,'rj'=2] {'ri'}, use_global_device_ids=true, to_apply=%region_7.8 | all-reduce | flops 2533 | bytes 20264 | tf_op jit(solution)/shard_map/psum | solution.py:176
  571.3 6.0 copy.188
  581.4 5.5 broadcast_select_fusion
  599.4 54.0 %all-reduce.7.cloned.1.call-done = (f32[3,3,64,64]{3,2,1,0:T(8,128)}, f32[3,3,64,64]{3,2,1,0:T(8,128)}) async-done(((f32[3,3,64,64]{3,2,1,0:T(8,128)}, f32[3,3,64,64]{3,2,1,0:T(8,128)}), (f32[3,3,64,64]{3,2,1,0:T(8,128)}, f32[3,3,64,64]{3,2,1,0:T(8,128)})) %all-reduce.7.cloned.1.call-update) | async-done | bytes 294928 | tf_op jit(solution)/shard_map/psum | solution.py:176
  (219 shorter events, 285.3 us)
Async XLA Ops:
  7.2 93.8 %copy-start = (bf16[3,3,64,64]{3,2,1,0:T(8,128)(2,1)S(1)}, bf16[3,3,64,64]{3,2,1,0:T(8,128)(2,1)}, u32[]{:S(2)}) copy-start(bf16[3,3,64,64]{3,2,1,0:T(8,128)(2,1)} %param.12) | copy-start | bytes 221188
  9.2 3.7 collective-permute-start
  11.5 5.5 collective-permute-start.1
  18.5 5.6 collective-permute-start.2
  22.2 6.6 collective-permute-start.3
  58.7 10.0 %collective-permute-start.4 = (bf16[64,8,256]{2,0,1:T(8,128)(2,1)}, bf16[64,8,256]{2,0,1:T(8,128)(2,1)}, u32[]{:S(2)}, u32[]{:S(2)}) collective-permute-start(bf16[64,8,256]{2,0,1:T(8,128)(2,1)} %get-tuple-element.65), channel_id=1, source_target_pairs={{0,2},{2,4},{4,6},{6,8},{8,10},{10,12},{12,14},{14,16},{16,18},{18... | collective-permute-start | bytes 786440 | tf_op jit(solution)/shard_map/ppermute | solution.py:18
  64.7 4.1 collective-permute-start.5
  73.6 7.1 %collective-permute-start.6 = (bf16[64,48,8]{0,2,1:T(8,128)(2,1)}, bf16[64,48,8]{0,2,1:T(8,128)(2,1)}, u32[]{:S(2)}, u32[]{:S(2)}) collective-permute-start(bf16[64,48,8]{0,2,1:T(8,128)(2,1)} %copy.150), channel_id=1, source_target_pairs={{0,1},{2,3},{4,5},{6,7},{8,9},{10,11},{12,13},{14,15},{16,17},{18,... | collective-permute-start | bytes 147464 | tf_op jit(solution)/shard_map/ppermute | solution.py:18
  78.0 6.8 %collective-permute-start.7 = (bf16[64,48,8]{0,2,1:T(8,128)(2,1)}, bf16[64,48,8]{0,2,1:T(8,128)(2,1)}, u32[]{:S(2)}, u32[]{:S(2)}) collective-permute-start(bf16[64,48,8]{0,2,1:T(8,128)(2,1)} %copy.151), channel_id=1, source_target_pairs={{1,0},{3,2},{5,4},{7,6},{9,8},{11,10},{13,12},{15,14},{17,16},{19,... | collective-permute-start | bytes 147464 | tf_op jit(solution)/shard_map/ppermute | solution.py:20
  116.5 16.7 %copy-start.6 = (bf16[64,32,256]{2,0,1:T(8,128)(2,1)}, bf16[64,32,256]{2,0,1:T(8,128)(2,1)S(1)}, u32[]{:S(2)}) copy-start(bf16[64,32,256]{2,0,1:T(8,128)(2,1)S(1)} %fusion.40) | copy-start | bytes 3145732
  191.8 19.3 %all-to-all-start.2 = ((bf16[2,2,131072]{2,1,0:T(2,128)(2,1)}), bf16[2,2,131072]{2,1,0:T(2,128)(2,1)}, u32[]{:S(2)}, u32[]{:S(2)}) async-start(bf16[2,2,131072]{2,1,0:T(2,128)(2,1)} %reshape.157), calls=%async_computation.2 | async-start | bytes 2097152 | tf_op jit(solution)/shard_map/all_to_all | solution.py:91
  267.3 45.5 %all-to-all-start.4 = ((f32[16,1,32768]{2,1,0:T(1,128)}), f32[16,1,32768]{2,1,0:T(1,128)}, u32[]{:S(2)}, u32[]{:S(2)}) async-start(f32[16,1,32768]{2,1,0:T(1,128)} %reshape.159), calls=%async_computation.4 | async-start | bytes 4194304 | tf_op jit(solution)/shard_map/all_to_all | solution.py:106
  337.0 31.0 %all-to-all-start.5 = ((f32[2,1,262144]{2,1,0:T(1,128)}), f32[2,1,262144]{2,1,0:T(1,128)}, u32[]{:S(2)}, u32[]{:S(2)}) async-start(f32[2,1,262144]{2,1,0:T(1,128)} %reshape.161), calls=%async_computation.5 | async-start | bytes 4194304 | tf_op jit(solution)/shard_map/all_to_all | solution.py:105
  341.8 221.3 %all-reduce.9.cloned.1.call-start = ((), (), s32[]{:S(2)}) async-start(), calls=%async_computation.7 | async-start | bytes 1179648 | tf_op jit(solution)/shard_map/psum | solution.py:177
  406.1 7.3 %collective-permute-start.8 = (bf16[64,8,256]{2,0,1:T(8,128)(2,1)S(1)}, bf16[64,8,256]{2,0,1:T(8,128)(2,1)S(1)}, u32[]{:S(2)}, u32[]{:S(2)}) collective-permute-start(bf16[64,8,256]{2,0,1:T(8,128)(2,1)S(1)} %get-tuple-element.63), channel_id=1, source_target_pairs={{0,2},{2,4},{4,6},{6,8},{8,10},{10,12},{12,14},{14,16},{16,18},{18... | collective-permute-start | bytes 786440 | tf_op jit(solution)/shard_map/ppermute | solution.py:18
  407.9 6.5 collective-permute-start.9
  416.2 15.7 %copy-start.2 = (bf16[64,32,256]{2,0,1:T(8,128)(2,1)S(1)}, bf16[64,32,256]{2,0,1:T(8,128)(2,1)}, u32[]{:S(2)}) copy-start(bf16[64,32,256]{2,0,1:T(8,128)(2,1)} %copy-done.1) | copy-start | bytes 3145732
  418.3 7.7 %collective-permute-start.10 = (bf16[64,48,8]{0,2,1:T(8,128)(2,1)}, bf16[64,48,8]{0,2,1:T(8,128)(2,1)}, u32[]{:S(2)}, u32[]{:S(2)}) collective-permute-start(bf16[64,48,8]{0,2,1:T(8,128)(2,1)} %copy.175), channel_id=1, source_target_pairs={{0,1},{2,3},{4,5},{6,7},{8,9},{10,11},{12,13},{14,15},{16,17},{18,... | collective-permute-start | bytes 147464 | tf_op jit(solution)/shard_map/ppermute | solution.py:18
  423.1 6.8 %collective-permute-start.11 = (bf16[64,48,8]{0,2,1:T(8,128)(2,1)}, bf16[64,48,8]{0,2,1:T(8,128)(2,1)}, u32[]{:S(2)}, u32[]{:S(2)}) collective-permute-start(bf16[64,48,8]{0,2,1:T(8,128)(2,1)} %copy.176), channel_id=1, source_target_pairs={{1,0},{3,2},{5,4},{7,6},{9,8},{11,10},{13,12},{15,14},{17,16},{19,... | collective-permute-start | bytes 147464 | tf_op jit(solution)/shard_map/ppermute | solution.py:20
  470.0 83.1 %collective-permute-start.12 = (bf16[64,8,256]{2,0,1:T(8,128)(2,1)S(1)}, bf16[64,8,256]{2,0,1:T(8,128)(2,1)S(1)}, u32[]{:S(2)}, u32[]{:S(2)}) collective-permute-start(bf16[64,8,256]{2,0,1:T(8,128)(2,1)S(1)} %get-tuple-element.61), channel_id=1, source_target_pairs={{0,2},{2,4},{4,6},{6,8},{8,10},{10,12},{12,14},{14,16},{16,18},{18... | collective-permute-start | bytes 786440 | tf_op jit(solution)/shard_map/ppermute | solution.py:18
  475.4 77.8 %collective-permute-start.13 = (bf16[64,8,256]{2,0,1:T(8,128)(2,1)S(1)}, bf16[64,8,256]{2,0,1:T(8,128)(2,1)S(1)}, u32[]{:S(2)}, u32[]{:S(2)}) collective-permute-start(bf16[64,8,256]{2,0,1:T(8,128)(2,1)S(1)} %get-tuple-element.62), channel_id=1, source_target_pairs={{2,0},{4,2},{6,4},{8,6},{10,8},{12,10},{14,12},{16,14},{18,16},{20... | collective-permute-start | bytes 786440 | tf_op jit(solution)/shard_map/ppermute | solution.py:20
  478.4 175.0 %all-reduce.7.cloned.1.call-start = ((), (), s32[]{:S(2)}) async-start(), calls=%async_computation.6 | async-start | bytes 1179648 | tf_op jit(solution)/shard_map/psum | solution.py:176
  557.5 5.6 collective-permute-start.14
  560.0 6.5 collective-permute-start.15
  (29 other events, 77.6 us)
Sparse Core Ops, SparseCore 0:
  478.6 37.5 all-reduce.8
  563.3 90.1 all-reduce.6
